TPU v7x, 256 devices: a whole 4x4x8 slice. The times are simulated.
256 devices in a mesh: expert: 32 (over z, y), tensor: 4 (over x), dp: 2 (over core).
Axes of the slice: x: 4, y: 4, z: 8, core: 2. Of those that a mesh axis runs over, the one named last changes fastest.
Arguments:
- tokens: bfloat16 [1024, 7168], P(('expert', 'dp')), may hold values from -6 to 6
- expert_ids: int32 [1024, 8], P(('expert', 'dp')), may hold values from 0 to 31, all different within a row; in each aligned block of 16 rows (0 to 15, 16 to 31, ...) at most 8 rows name the same one
- route_scores: float32 [1024, 8], P(('expert', 'dp')), may hold values from 0.05 to 1
- gate_weight: bfloat16 [32, 7168, 2048], P('expert', 'dp', 'tensor'), may hold values from -0.0625 to 0.0625
- up_weight: bfloat16 [32, 7168, 2048], P('expert', 'dp', 'tensor'), may hold values from -0.0625 to 0.0625
- down_weight: bfloat16 [32, 2048, 7168], P('expert', 'tensor', 'dp'), may hold values from -0.125 to 0.125
Outputs:
- mixed: bfloat16 [1024, 2, 3584], P(('expert', 'dp'), None, 'tensor')
Inputs may be any that keep to these rules, and one draw needn't show every extreme that they name: `expert_ids`: each token names 8 different experts. In each aligned block of 16 tokens (the tokens of one device along expert and dp) no expert is named by more than 8 tokens, a bound that some block reaches.
All inputs are finite; a program needn't handle non-finite values.
Results may differ from a plain program's by a relative error of at most 0.02.
Values may be sent and summed in bfloat16 or wider, within the bound.
A program may use at most 64 MiB of HBM per device.

v0:
```python
import jax
import jax.numpy as jnp
from jax import lax
from jax.sharding import PartitionSpec as P

TOP = 8
EXPERTS = 32
CAP = 8


def route_over_experts(blocks):
    return lax.all_to_all(blocks, "expert", split_axis=2, concat_axis=2, tiled=True)


def block_tables(block_ids, expert_count):
    pair_ids = block_ids.reshape(-1)
    expert_hot = (pair_ids[:, None] == jnp.arange(EXPERTS, dtype=jnp.int32)[None, :]).astype(
        jnp.int32
    )
    earlier = jnp.cumsum(expert_hot, axis=0) - expert_hot
    slot_index = jnp.sum(earlier * expert_hot, axis=1).reshape(block_ids.shape)
    expert_onehot = (
        block_ids[:, :, None] == jnp.arange(EXPERTS, dtype=jnp.int32)[None, None, :]
    ).astype(jnp.float32)
    expert_onehot = expert_onehot.reshape(
        block_ids.shape[0], TOP, expert_count, EXPERTS // expert_count
    )
    slot_onehot = (
        slot_index[:, :, None] == jnp.arange(CAP, dtype=jnp.int32)[None, None, :]
    ).astype(jnp.float32)
    return (expert_onehot, slot_onehot)


def placing_table(block_ids, expert_count):
    expert_onehot, slot_onehot = block_tables(block_ids, expert_count)
    return jnp.einsum("tkgl,tkc->lgct", expert_onehot, slot_onehot).astype(jnp.bfloat16)


def mixing_table(block_ids, block_scores, expert_count):
    expert_onehot, slot_onehot = block_tables(block_ids, expert_count)
    weights = (2.5 * block_scores / jnp.sum(block_scores, axis=1, keepdims=True)).astype(
        jnp.bfloat16
    )
    return jnp.einsum(
        "tk,tkgl,tkc->tglc", weights.astype(jnp.float32), expert_onehot, slot_onehot
    ).astype(jnp.bfloat16)


def on_device(tokens, expert_ids, route_scores, gate_weight, up_weight, down_weight):
    expert_count = lax.axis_size("expert")
    dp_count = lax.axis_size("dp")
    local_experts = gate_weight.shape[0]
    block_tokens = expert_ids.shape[0]
    placing = placing_table(expert_ids, expert_count)
    split_rows = tokens.reshape(block_tokens, dp_count, tokens.shape[1] // dp_count)
    outgoing = jnp.einsum(
        "lgct,tpd->lpgcd", placing, split_rows, preferred_element_type=jnp.float32
    ).astype(jnp.bfloat16)
    halves = lax.all_to_all(outgoing, "dp", split_axis=1, concat_axis=1, tiled=True)
    half_width = halves.shape[4]
    arrived = route_over_experts(halves)
    arrived = arrived.reshape(local_experts, dp_count * expert_count * CAP, half_width)
    gate = jnp.einsum("lrh,lhf->lrf", arrived, gate_weight, preferred_element_type=jnp.float32)
    up = jnp.einsum("lrh,lhf->lrf", arrived, up_weight, preferred_element_type=jnp.float32)
    gate, up = (
        lax.psum(gate.astype(jnp.bfloat16), "dp").astype(jnp.float32),
        lax.psum(up.astype(jnp.bfloat16), "dp").astype(jnp.float32),
    )
    hidden = (jax.nn.silu(gate) * up).astype(jnp.bfloat16)
    partial_value = jnp.einsum(
        "lrf,lfh->lrh", hidden, down_weight, preferred_element_type=jnp.float32
    )
    summed = lax.psum_scatter(
        partial_value.astype(jnp.bfloat16), "tensor", scatter_dimension=2, tiled=True
    ).astype(jnp.float32)
    summed = summed.astype(jnp.bfloat16).reshape(
        local_experts, dp_count, expert_count, CAP, summed.shape[2]
    )
    returned = route_over_experts(summed)
    results = lax.all_to_all(returned, "dp", split_axis=1, concat_axis=1, tiled=True)
    mixing = mixing_table(expert_ids, route_scores, expert_count)
    mixed = jnp.einsum("tglc,lhgcd->thd", mixing, results, preferred_element_type=jnp.float32)
    return mixed.astype(jnp.bfloat16)


def solution(mesh):
    in_specs = (
        P(("expert", "dp"), None),
        P(("expert", "dp"), None),
        P(("expert", "dp"), None),
        P("expert", "dp", "tensor"),
        P("expert", "dp", "tensor"),
        P("expert", "tensor", "dp"),
    )
    out_specs = P(("expert", "dp"), None, "tensor")
    return jax.shard_map(
        on_device, mesh=mesh, in_specs=in_specs, out_specs=out_specs, check_vma=False
    )
```

profile of v0, /device:TPU:1, one launch (start us, length us, event | category | flops | bytes accessed | tf_op | source)
XLA Modules:
  0.0 278.3 jit_solution(17216406574727778507)
XLA Ops:
  6.5 0.0 all-reduce.3.cloned.1.call-start
  6.5 0.8 copy.22
  7.3 0.1 eq.28
  7.4 0.1 fusion.31
  7.5 0.2 reduce_window_sum.12
  7.7 0.2 select_reduce_fusion
  7.8 0.1 eq.32
  7.9 0.2 fusion.20
  8.1 0.1 copy.34
  8.3 2.0 fusion
  10.3 0.3 copy.27
  10.6 9.6 %all_to_all.20 = bf16[1,2,32,8,3584]{4,3,2,0,1:T(8,128)(2,1)S(1)} all-to-all(bf16[1,2,32,8,3584]{4,3,2,0,1:T(8,128)(2,1)S(1)} %copy.27), channel_id=1, replica_groups=mesh['expert'=32,'tensor'=4,'dp'=2] {'dp'}, dimensions={1} | all-to-all | bytes 7340032 | tf_op jit(solution)/shard_map/all_to_all | solution.py:59
  20.1 0.5 copy.28
  20.6 93.1 %all_to_all.21 = bf16[1,2,32,8,3584]{4,3,1,0,2:T(8,128)(2,1)S(1)} all-to-all(bf16[1,2,32,8,3584]{4,3,1,0,2:T(8,128)(2,1)S(1)} %copy.28), channel_id=1, replica_groups=mesh['expert'=32,'tensor'=4,'dp'=2] {'expert'}, dimensions={2} | all-to-all | bytes 7340032 | tf_op jit(solution)/shard_map/all_to_all | solution.py:12
  113.7 0.0 copy-start.1
  113.7 0.3 copy.29
  114.0 1.8 copy-done.1
  115.8 0.0 copy-start.2
  115.8 2.9 %fusion.13 = bf16[1,512,512]{2,1,0:T(8,128)(2,1)} fusion(bf16[512,3584]{1,0:T(8,128)(2,1)S(1)} %bitcast.71, bf16[1,3584,512]{2,1,0:T(8,128)(2,1)S(1)} %copy-done.1), kind=kOutput, calls=%fused_computation.15 | convolution fusion | flops 1879310336 | bytes 7864320 | tf_op jit(solution)/shard_map/lrh,lhf->lrf/dot_general | solution.py:64
  118.6 0.0 copy-done.2
  118.6 2.9 %fusion.16 = bf16[1,512,512]{2,1,0:T(8,128)(2,1)} fusion(bf16[512,3584]{1,0:T(8,128)(2,1)S(1)} %bitcast.72, bf16[1,3584,512]{2,1,0:T(8,128)(2,1)S(1)} %copy-done.2), kind=kOutput, calls=%fused_computation.16 | convolution fusion | flops 1879310336 | bytes 7864320 | tf_op jit(solution)/shard_map/lrh,lhf->lrf/dot_general | solution.py:63
  121.5 0.0 all-reduce.3.cloned.1.call-update
  121.6 0.0 reduce-scatter.4.cloned.1.call-start
  121.6 29.0 %all-reduce.3.cloned.1.call-done = (bf16[1,512,512]{2,1,0:T(8,128)(2,1)}, bf16[1,512,512]{2,1,0:T(8,128)(2,1)}) async-done(((bf16[1,512,512]{2,1,0:T(8,128)(2,1)}, bf16[1,512,512]{2,1,0:T(8,128)(2,1)}), (bf16[1,512,512]{2,1,0:T(8,128)(2,1)}, bf16[1,512,512]{2,1,0:T(8,128)(2,1)})) %all-reduce.3.cloned.1.call-update) | async-done | bytes 1048592 | tf_op jit(solution)/shard_map/psum | solution.py:67
  150.6 6.4 %fusion.1 = bf16[1,512,3584]{2,1,0:T(8,128)(2,1)} fusion(bf16[1,512,3584]{2,1,0:T(8,128)(2,1)} %param.11, bf16[1,512,512]{2,1,0:T(8,128)(2,1)} %get-tuple-element.5, bf16[1,512,512]{2,1,0:T(8,128)(2,1)} %get-tuple-element.6), kind=kOutput, calls=%fused_computation.3 | convolution fusion | flops 1882980352 | bytes 8388608 | tf_op jit(solution)/shard_map/lrf,lfh->lrh/dot_general | solution.py:70
  157.0 16.5 %copy.38 = bf16[1,512,3584]{1,0,2:T(2,128)(2,1)} copy(bf16[1,512,3584]{2,1,0:T(8,128)(2,1)} %fusion.1) | data formatting | bytes 7340032
  173.5 6.1 %copy.51 = bf16[3584,1,512]{2,0,1:T(8,128)(2,1)} copy(bf16[3584,1,512]{2,1,0:T(2,128)(2,1)} %bitcast.69) | data formatting | bytes 7340032
  179.6 0.0 reduce-scatter.4.cloned.1.call-update
  179.6 45.8 %reduce-scatter.4.cloned.1.call-done = bf16[896,512]{1,0:T(8,128)(2,1)} async-done(((bf16[3584,512]{1,0:T(8,128)(2,1)}), bf16[896,512]{1,0:T(8,128)(2,1)}) %reduce-scatter.4.cloned.1.call-update) | async-done | bytes 917520
  225.5 2.1 reshape_bitcast_fusion
  227.6 0.0 copy-start
  227.6 1.3 copy.39
  228.9 1.0 copy.30
  229.9 9.6 %all-to-all-start.2 = ((bf16[1,2,32,8,896]{4,3,1,0,2:T(8,128)(2,1)}), bf16[1,2,32,8,896]{4,3,1,0,2:T(8,128)(2,1)S(1)}, u32[]{:S(2)}, u32[]{:S(2)}) async-start(bf16[1,2,32,8,896]{4,3,1,0,2:T(8,128)(2,1)} %copy.30), calls=%async_computation.2 | async-start | bytes 1835008 | tf_op jit(solution)/shard_map/all_to_all | solution.py:12
  239.5 0.0 copy-done
  239.5 0.1 copy.24
  239.6 0.2 convolution_convert_fusion.3
  239.8 23.1 %all-to-all-done.2 = bf16[1,2,32,8,896]{4,3,1,0,2:T(8,128)(2,1)S(1)} async-done(((bf16[1,2,32,8,896]{4,3,1,0,2:T(8,128)(2,1)}), bf16[1,2,32,8,896]{4,3,1,0,2:T(8,128)(2,1)S(1)}, u32[]{:S(2)}, u32[]{:S(2)}) %all-to-all-start.2) | async-done | bytes 917536 | tf_op jit(solution)/shard_map/all_to_all | solution.py:12
  263.0 0.2 copy.31
  263.1 7.2 %all_to_all.22 = bf16[1,2,32,8,896]{4,2,3,0,1:T(8,128)(2,1)S(1)} all-to-all(bf16[1,2,32,8,896]{4,2,3,0,1:T(8,128)(2,1)S(1)} %copy.31), channel_id=1, replica_groups=mesh['expert'=32,'tensor'=4,'dp'=2] {'dp'}, dimensions={1} | all-to-all | bytes 1835008 | tf_op jit(solution)/shard_map/all_to_all | solution.py:80
  270.3 0.4 fusion.19
  270.8 0.7 copy.33
  (2 shorter events, 0.0 us)
Async XLA Ops:
  6.5 144.1 %all-reduce.3.cloned.1.call-start = ((), (), s32[]{:S(2)}) async-start(), calls=%async_computation.6 | async-start | bytes 2097152 | tf_op jit(solution)/shard_map/psum | solution.py:67
  113.7 2.0 copy-start.1
  115.8 2.9 %copy-start.2 = (bf16[1,3584,512]{2,1,0:T(8,128)(2,1)S(1)}, bf16[1,3584,512]{2,1,0:T(8,128)(2,1)}, u32[]{:S(2)}) copy-start(bf16[1,3584,512]{2,1,0:T(8,128)(2,1)} %param.9) | copy-start | bytes 11010052
  121.6 103.9 %reduce-scatter.4.cloned.1.call-start = ((), (), s32[]{:S(2)}) async-start(), calls=%async_computation.5 | async-start | bytes 4587520
  227.6 11.9 %copy-start = (f32[16,8]{0,1:T(8,128)S(1)}, f32[16,8]{0,1:T(8,128)}, u32[]{:S(2)}) copy-start(f32[16,8]{0,1:T(8,128)} %param.8) | copy-start | bytes 1540
  229.9 33.1 %all-to-all-start.2 = ((bf16[1,2,32,8,896]{4,3,1,0,2:T(8,128)(2,1)}), bf16[1,2,32,8,896]{4,3,1,0,2:T(8,128)(2,1)S(1)}, u32[]{:S(2)}, u32[]{:S(2)}) async-start(bf16[1,2,32,8,896]{4,3,1,0,2:T(8,128)(2,1)} %copy.30), calls=%async_computation.2 | async-start | bytes 1835008 | tf_op jit(solution)/shard_map/all_to_all | solution.py:12
Sparse Core Ops, SparseCore 0:
  121.7 28.8 all-reduce.2
  179.7 45.6 reduce-scatter.3
where the time goes:
time: 279 us; the launch traced here: 278 us
  blocking collectives  110 us (39%)
  waiting for transfers between devices  98 us (35%)
  local copies, waits for them, and re-layouts  31.8 us (11%)
  matrix products  15.1 us (5%)
  between operations  13.5 us (5%)
  starting transfers between devices  9.6 us (3%)
    all_to_all x1, blocking collectives, route_over_experts(): lax.all_to_all(blocks, 'expert', split_axis=2, concat_axis=2, tiled=True)  93.1 us
    unnamed x3, waiting for transfers between devices  45.9 us
    psum x1, waiting for transfers between devices, on_device(): lax.psum(up.astype(jnp.bfloat16), 'dp').astype(jnp.float32)  29 us
    unnamed x11, local copies, waits for them, and re-layouts  28.5 us
    all_to_all x1, waiting for transfers between devices, route_over_experts(): lax.all_to_all(blocks, 'expert', split_axis=2, concat_axis=2, tiled=True)  23.1 us
    all_to_all x1, starting transfers between devices, route_over_experts(): lax.all_to_all(blocks, 'expert', split_axis=2, concat_axis=2, tiled=True)  9.56 us
    all_to_all x1, blocking collectives, on_device(): lax.all_to_all(outgoing, 'dp', split_axis=1, concat_axis=1, tiled=True)  9.55 us
    all_to_all x1, blocking collectives, on_device(): lax.all_to_all(returned, 'dp', split_axis=1, concat_axis=1, tiled=True)  7.17 us
  transfers between devices with their start and end apart: 3, of which 3 were waited for; matrix products, arithmetic and copies ran while one was open for 0% of the time, Pallas kernels for 0%

commit v1 on v0

v1 whole, which is shorter than its diff:
```python
import jax
import jax.numpy as jnp
from jax import lax
from jax.experimental import pallas as pl
from jax.experimental.pallas import tpu as pltpu
from jax.sharding import PartitionSpec as P

MESH = pl.DeviceIdType.MESH
BF16 = jnp.bfloat16
F32 = jnp.float32
TOP = 8
CAP = 8
BLOCK = 16
NZ, NY, NX = 8, 4, 4
HALF = 3584
Q = 896
W2 = 2 * Q
FFQ = 512
ROWS = 512
ORDER = (0, 1, -1, 2, -2, 3, -3, 4)
GROUPS = ((0,), (1, -1), (2, -2), (3, -3), (4,))
START = (0, 1, 3, 5, 7)
NG = len(GROUPS)
N_REMOTE = 128
N_LOCAL = 32


def place_of(offset):
    return ORDER.index((offset + 3) % NZ - 3)


def kernel(
    tokens, ids, scores, wg_hbm, wu_hbm, wd_hbm, out,
    w_gu, w_d, tok, slots, relay, x, own_gu, send_gu, recv_gu, hid, y, xr, zsum, yr, relay2,
    mix, zs, zr, f_own, f_send, f_recv,
    send_sem, recv_sem, local_sem,
):
    e_id, t, d = lax.axis_index("expert"), lax.axis_index("tensor"), lax.axis_index("dp")
    zi, yi = e_id // NY, e_id % NY
    par = t % 2

    def at_z(offset):
        return {"expert": lax.rem(zi + NZ + offset, NZ) * NY + yi, "tensor": t, "dp": d}

    def at_y(offset):
        return {"expert": zi * NY + lax.rem(yi + NY + offset, NY), "tensor": t, "dp": d}

    def at_x(offset, core):
        return {"expert": e_id, "tensor": lax.rem(t + NX + offset, NX), "dp": core}

    remote, local = {}, {}

    def send(key, src, dst, device):
        n = len(remote)
        copy = pltpu.make_async_remote_copy(
            src_ref=src, dst_ref=dst, send_sem=send_sem.at[n], recv_sem=recv_sem.at[n],
            device_id=device, device_id_type=MESH,
        )
        copy.start()
        remote[key] = copy

    def arrived(key):
        remote[key].wait_recv()

    def move(key, src, dst):
        copy = pltpu.make_async_copy(src, dst, local_sem.at[len(local)])
        copy.start()
        local[key] = copy

    def quarter(q):
        return pl.ds(pl.multiple_of(q * Q, 128), Q)

    def half_quarter(half, q):
        return pl.ds(pl.multiple_of(half * HALF + q * Q, 128), Q)

    def block_rows(b):
        return pl.ds(pl.multiple_of(b * BLOCK, BLOCK), BLOCK)

    barrier = pltpu.get_barrier_semaphore()
    peers = [at_z(o) for o in range(1, NZ)] + [at_y(1), at_y(-1), at_x(1, d), at_x(-1, d)]
    peers += [at_x(2, d), at_x(2, 1 - d), at_x(0, 1 - d)]
    for peer in peers:
        pl.semaphore_signal(barrier, inc=1, device_id=peer, device_id_type=MESH)

    move("wg", wg_hbm, w_gu.at[:, pl.ds(0, FFQ)])
    move("wu", wu_hbm, w_gu.at[:, pl.ds(FFQ, FFQ)])
    move("wd", wd_hbm, w_d)
    mine = block_rows(d)
    move("t0", tokens.at[:, half_quarter(d, par)], tok.at[mine, pl.ds(0, Q)])
    move("t1", tokens.at[:, half_quarter(d, par + 2)], tok.at[mine, pl.ds(Q, Q)])

    lane = lax.broadcasted_iota(jnp.int32, (BLOCK, 128), 1)
    chosen, rs = ids[...], scores[...]
    w = (2.5 * rs / jnp.sum(rs, axis=1, keepdims=True)).astype(BF16).astype(F32)
    hot = jnp.zeros((BLOCK, 128), F32)
    weight = jnp.zeros((BLOCK, 128), F32)
    for k in range(TOP):
        ek = chosen[:, k:k + 1]
        hot += jnp.where(ek == lane, 1.0, 0.0)
        weight += jnp.where(ek + 32 == lane, w[:, k:k + 1], 0.0)
    lower = jnp.where(
        lax.broadcasted_iota(jnp.int32, (BLOCK, BLOCK), 0)
        > lax.broadcasted_iota(jnp.int32, (BLOCK, BLOCK), 1), 1.0, 0.0)
    earlier = jnp.dot(lower.astype(BF16), hot.astype(BF16), preferred_element_type=F32)
    table = jnp.where(hot > 0.0, earlier + 1.0, 0.0) + weight
    tok[mine, pl.ds(W2, 128)] = table.astype(BF16)

    pl.semaphore_wait(barrier, len(peers))

    other = at_x(0, 1 - d)
    send("d0", tokens.at[:, half_quarter(1 - d, par)], tok.at[mine, pl.ds(0, Q)], other)
    send("d1", tokens.at[:, half_quarter(1 - d, par + 2)], tok.at[mine, pl.ds(Q, Q)], other)
    send("d2", tok.at[mine, pl.ds(W2, 128)], tok.at[mine, pl.ds(W2, 128)], other)
    for k in ("t0", "t1"):
        local[k].wait()
    for k in ("d0", "d1", "d2"):
        arrived(k)

    def chunk(offset, first=0, count=32):
        return tok.at[pl.ds(32 * place_of(offset) + first, count)]

    def span(g):
        n = len(GROUPS[g])
        return n, 64 * START[g], 16 * n

    def gather_and_place(g):
        n, base, m = span(g)
        if g == 0:
            send(("z", -1), chunk(0), chunk(-1), at_z(1))
            send(("z", 1), chunk(0), chunk(1), at_z(-1))
        elif g < 4:
            for o in GROUPS[g]:
                arrived(("z", o))
            if g < 3:
                send(("z", -g - 1), chunk(-g), chunk(-g - 1), at_z(1))
                send(("z", g + 1), chunk(g), chunk(g + 1), at_z(-1))
            else:
                send(("z", "a"), chunk(-3, 0, 16), chunk(4, 0, 16), at_z(1))
                send(("z", "b"), chunk(3, 16, 16), chunk(4, 16, 16), at_z(-1))
        else:
            arrived(("z", "a"))
            arrived(("z", "b"))
        first = 32 * START[g]
        tab = tok[first:first + 32 * n, W2:]
        col = lax.broadcasted_iota(jnp.int32, (128, 4 * m), 1)
        src = lax.broadcasted_iota(jnp.int32, (128, 4 * m), 0)
        expert = zi * NY + (yi + col // m) % NY
        slot_of = jnp.dot(tab, jnp.where(src == expert, 1.0, 0.0).astype(BF16),
                          preferred_element_type=F32)
        weight_of = jnp.dot(tab, jnp.where(src == expert + 32, 1.0, 0.0).astype(BF16),
                            preferred_element_type=F32)
        c2 = lax.broadcasted_iota(jnp.int32, (32 * n, 4 * m), 1)
        r2 = lax.broadcasted_iota(jnp.int32, (32 * n, 4 * m), 0)
        want = (c2 % CAP + 1).astype(F32)
        hit = (slot_of == want) & ((c2 % m) // CAP == r2 // BLOCK)
        placing = jnp.where(hit, 1.0, 0.0).astype(BF16)
        mix[first:first + 32 * n, 0:4 * m] = jnp.where(hit, weight_of, 0.0).astype(BF16)
        rows = lax.dot_general(
            placing, tok[first:first + 32 * n, 0:W2], (((0,), (0,)), ((), ())),
            preferred_element_type=F32)
        slots[base:base + 4 * m, :] = rows.astype(BF16)
        lo, hi = pl.ds(0, Q), pl.ds(Q, Q)
        qs = (quarter(par), quarter(par + 2))

        def part(j, half):
            return slots.at[pl.ds(base + j * m, m), half]

        def place(c, k):
            return x.at[pl.ds(base + c * m, m), qs[k]]

        rl = pl.ds(16 * START[g], m)
        send(("r", g, 0), part(2, lo), relay.at[0, rl], at_y(1))
        send(("r", g, 1), part(2, hi), relay.at[1, rl], at_y(-1))
        for k, half in enumerate((lo, hi)):
            send(("y1", g, k), part(1, half), place(3, k), at_y(1))
            send(("y3", g, k), part(3, half), place(1, k), at_y(-1))
            move(("y0", g, k), part(0, half), place(0, k))

    def relay_rows(g):
        n, base, m = span(g)
        rl = pl.ds(16 * START[g], m)
        qs = (quarter(par), quarter(par + 2))
        for k, step in ((0, 1), (1, -1)):
            arrived(("r", g, k))
            send(("y2", g, k), relay.at[k, rl], x.at[pl.ds(base + 2 * m, m), qs[k]], at_y(step))

    def swap_halves(g):
        n, base, m = span(g)
        for k in range(2):
            local[("y0", g, k)].wait()
            for kind in ("y1", "y3", "y2"):
                arrived((kind, g, k))
        rows = pl.ds(base, 4 * m)
        for k, step in ((0, 1), (1, -1)):
            view = x.at[rows, quarter(par + 2 * k)]
            send(("x", g, k), view, view, at_x(step, d))

    def gate_up(g):
        n, base, m = span(g)
        if g == 0:
            local["wg"].wait()
            local["wu"].wait()
        for k in range(2):
            arrived(("x", g, k))

        def tile(i, carry):
            cols = pl.ds(pl.multiple_of(i * 256, 256), 256)
            part = jnp.dot(x[base:base + 4 * m, :], w_gu[:, cols], preferred_element_type=F32)
            own_gu[g % 2, 0:4 * m, cols] = part
            send_gu[base:base + 4 * m, cols] = part.astype(BF16)
            return carry

        lax.fori_loop(0, 2 * FFQ // 256, tile, 0)
        rows = pl.ds(base, 4 * m)
        send(("gu", g), send_gu.at[rows], recv_gu.at[rows], at_x(0, 1 - d))

    def down(g):
        n, base, m = span(g)
        if g == 0:
            local["wd"].wait()
        arrived(("gu", g))
        total = own_gu[g % 2, 0:4 * m, :] + recv_gu[base:base + 4 * m, :].astype(F32)
        gate, up = total[:, :FFQ], total[:, FFQ:]
        hid[0:4 * m, :] = (gate / (1.0 + jnp.exp(-gate)) * up).astype(BF16)

        def tile(i, carry):
            cols = pl.ds(pl.multiple_of(i * 512, 512), 512)
            part = jnp.dot(hid[0:4 * m, :], w_d[:, cols], preferred_element_type=F32)
            y[base:base + 4 * m, cols] = part.astype(BF16)
            return carry

        lax.fori_loop(0, HALF // 512, tile, 0)
        rows = pl.ds(base, 4 * m)
        send(("xr", g, 0), y.at[rows, quarter(1 - par)], xr.at[0, rows], at_x(-1, d))
        send(("xr", g, 1), y.at[rows, quarter(3 - par)], xr.at[1, rows], at_x(1, d))

    def add_and_return(g):
        n, base, m = span(g)
        for k in range(2):
            arrived(("xr", g, k))
            mine_y = y[base:base + 4 * m, quarter(par + 2 * k)].astype(F32)
            zsum[base:base + 4 * m, k * Q:(k + 1) * Q] = (
                mine_y + xr[k, base:base + 4 * m, :].astype(F32)).astype(BF16)
        lo, hi = pl.ds(0, Q), pl.ds(Q, Q)
        rl = pl.ds(16 * START[g], m)

        def rows(c):
            return pl.ds(base + c * m, m)

        send(("s", g, 0), zsum.at[rows(2), lo], relay2.at[0, rl], at_y(1))
        send(("s", g, 1), zsum.at[rows(2), hi], relay2.at[1, rl], at_y(-1))
        send(("v1", g), zsum.at[rows(1)], yr.at[rows(3)], at_y(1))
        send(("v3", g), zsum.at[rows(3)], yr.at[rows(1)], at_y(-1))
        move(("v0", g), zsum.at[rows(0)], yr.at[rows(0)])

    def relay_results(g):
        n, base, m = span(g)
        rl = pl.ds(16 * START[g], m)
        rows = pl.ds(base + 2 * m, m)
        for k, step in ((0, 1), (1, -1)):
            arrived(("s", g, k))
            send(("v2", g, k), relay2.at[k, rl], yr.at[rows, pl.ds(k * Q, Q)], at_y(step))

    def combine(g):
        n, base, m = span(g)
        local[("v0", g)].wait()
        for key in (("v1", g), ("v3", g), ("v2", g, 0), ("v2", g, 1)):
            arrived(key)
        first = 32 * START[g]
        part = jnp.dot(mix[first:first + 32 * n, 0:4 * m], yr[base:base + 4 * m, :],
                       preferred_element_type=F32)
        zs[first:first + 32 * n, :] = part.astype(BF16)
        for o in GROUPS[g]:
            if o:
                send(("w", o), zs.at[pl.ds(32 * place_of(o), 32)],
                     zr.at[pl.ds(32 * place_of(-o), 32)], at_z(o))

    stages = (
        (gather_and_place, 0), (gate_up, 2), (relay_rows, 0), (down, 2),
        (add_and_return, 3), (swap_halves, 0), (relay_results, 3), (combine, 4),
    )
    for s in range(NG + 4):
        for stage, lag in stages:
            if 0 <= s - lag < NG:
                stage(s - lag)

    total = zs[0:32, :].astype(F32)
    for o in ORDER[1:]:
        arrived(("w", o))
    for i in range(1, NZ):
        total += zr[32 * i:32 * (i + 1), :].astype(F32)
    low = jnp.broadcast_to(t < 2, (32, Q))
    f_own[...] = jnp.where(low, total[:, :Q], total[:, Q:])
    f_send[0] = f_own[...].astype(BF16)
    f_send[1] = jnp.where(low, total[:, Q:], total[:, :Q]).astype(BF16)
    theirs = block_rows(1 - d)
    send("f0", f_send.at[0, theirs], f_recv.at[0], at_x(0, 1 - d))
    send("f1", f_send.at[1, mine], f_recv.at[1], at_x(2, d))
    send("f2", f_send.at[1, theirs], f_recv.at[2], at_x(2, 1 - d))
    for k in ("f0", "f1", "f2"):
        arrived(k)
    out[d] = (f_own[mine, :] + f_recv[1].astype(F32)).astype(BF16)
    out[1 - d] = (f_recv[0].astype(F32) + f_recv[2].astype(F32)).astype(BF16)
    for copy in remote.values():
        copy.wait_send()


def on_device(tokens, expert_ids, route_scores, gate_weight, up_weight, down_weight):
    vmem = pl.BlockSpec(memory_space=pltpu.VMEM)
    hbm = pl.BlockSpec(memory_space=pl.ANY)
    scratch = [
        pltpu.VMEM((HALF, 2 * FFQ), BF16),
        pltpu.VMEM((FFQ, HALF), BF16),
        pltpu.VMEM((32 * NZ, W2 + 128), BF16),
        pltpu.VMEM((ROWS, W2), BF16),
        pltpu.VMEM((2, 16 * NZ, Q), BF16),
        pltpu.VMEM((ROWS, HALF), BF16),
        pltpu.VMEM((2, 128, 2 * FFQ), F32),
        pltpu.VMEM((ROWS, 2 * FFQ), BF16),
        pltpu.VMEM((ROWS, 2 * FFQ), BF16),
        pltpu.VMEM((128, FFQ), BF16),
        pltpu.VMEM((ROWS, HALF), BF16),
        pltpu.VMEM((2, ROWS, Q), BF16),
        pltpu.VMEM((ROWS, W2), BF16),
        pltpu.VMEM((ROWS, W2), BF16),
        pltpu.VMEM((2, 16 * NZ, Q), BF16),
        pltpu.VMEM((32 * NZ, 128), BF16),
        pltpu.VMEM((32 * NZ, W2), BF16),
        pltpu.VMEM((32 * NZ, W2), BF16),
        pltpu.VMEM((32, Q), F32),
        pltpu.VMEM((2, 32, Q), BF16),
        pltpu.VMEM((3, BLOCK, Q), BF16),
        pltpu.SemaphoreType.DMA((N_REMOTE,)),
        pltpu.SemaphoreType.DMA((N_REMOTE,)),
        pltpu.SemaphoreType.DMA((N_LOCAL,)),
    ]
    out = pl.pallas_call(
        kernel,
        out_shape=jax.ShapeDtypeStruct((2, BLOCK, Q), BF16),
        in_specs=[vmem, vmem, vmem, hbm, hbm, hbm],
        out_specs=vmem,
        scratch_shapes=scratch,
        compiler_params=pltpu.CompilerParams(
            collective_id=0, has_side_effects=True, vmem_limit_bytes=60 * 1024 * 1024
        ),
    )(tokens, expert_ids, route_scores, gate_weight[0], up_weight[0], down_weight[0])
    return out.transpose(1, 0, 2)


def solution(mesh):
    in_specs = (
        P(("expert", "dp"), None),
        P(("expert", "dp"), None),
        P(("expert", "dp"), None),
        P("expert", "dp", "tensor"),
        P("expert", "dp", "tensor"),
        P("expert", "tensor", "dp"),
    )
    out_specs = P(("expert", "dp"), None, "tensor")
    return jax.shard_map(
        on_device, mesh=mesh, in_specs=in_specs, out_specs=out_specs, check_vma=False
    )
```

time: 279 us -> 106 us (0.38)
  blocking collectives: 110 us -> 0 us
  Pallas kernels: 0 us -> 102 us
  waiting for transfers between devices: 98 us -> 0 us
  local copies, waits for them, and re-layouts: 31.8 us -> 4.19 us
  matrix products: 15.1 us -> 0 us
  between operations: 13.5 us -> 0.01 us
  starting transfers between devices: 9.6 us -> 0 us
    all_to_all x3 -> x0, blocking collectives: 110 us -> none  [the longest x1 93.1 us: route_over_experts(): lax.all_to_all(blocks, 'expert', split_axis=2, concat_axis=2, tiled=True)]
    pallas_call x0 -> x1, Pallas kernels: none -> 102 us  [on_device(): pl.pallas_call(kernel, out_shape=jax.ShapeDtypeStruct((2, BLOCK, Q), BF16...]
    unnamed x3 -> x0, waiting for transfers between devices: 45.9 us -> none
    psum x1 -> x0, waiting for transfers between devices: 29 us -> none  [on_device(): lax.psum(up.astype(jnp.bfloat16), 'dp').astype(jnp.float32)]
    unnamed x11 -> x2, local copies, waits for them, and re-layouts: 28.5 us -> 2.7 us
    all_to_all x1 -> x0, waiting for transfers between devices: 23.1 us -> none  [route_over_experts(): lax.all_to_all(blocks, 'expert', split_axis=2, concat_axis=2, tiled=True)]
    dot_general x7 -> x0, matrix products: 15.1 us -> none  [the longest x1 6.42 us: on_device(): jnp.einsum('lrf,lfh->lrh', hidden, down_weight, preferred_element_type=jn...]
    all_to_all x1 -> x0, starting transfers between devices: 9.56 us -> none  [route_over_experts(): lax.all_to_all(blocks, 'expert', split_axis=2, concat_axis=2, tiled=True)]
  transfers between devices with their start and end apart: 3 -> 0, of which waited for: 3 -> 0; matrix products, arithmetic and copies ran while one was open for 0% -> 0% of each run, Pallas kernels for 0% -> 0%
where the time goes in v1:
time: 106 us
  Pallas kernels  102 us (96%)
  local copies, waits for them, and re-layouts  4.19 us (4%)
    pallas_call x1, Pallas kernels, on_device(): pl.pallas_call(kernel, out_shape=jax.ShapeDtypeStruct((2, BLOCK, Q), BF16...  102 us
    unnamed x2, local copies, waits for them, and re-layouts  2.7 us

profile of v1, /device:TPU:1, one launch (start us, length us, event | category | flops | bytes accessed | tf_op | source)
XLA Modules:
  0.0 105.8 jit_solution(8754555308575121259)
XLA Ops:
  0.0 1.4 %copy.7.ids = s32[16,8]{1,0:T(8,128)} copy(s32[16,8]{0,1:T(8,128)} %param.7) | data formatting | bytes 1024 | tf_op args[1]
  1.4 1.3 %copy.8.scores = f32[16,8]{1,0:T(8,128)} copy(f32[16,8]{0,1:T(8,128)} %param.8) | data formatting | bytes 1024 | tf_op args[2]
  2.7 101.6 %shard_map.64 = bf16[2,16,896]{2,1,0:T(8,128)(2,1)} custom-call(bf16[16,7168]{1,0:T(8,128)(2,1)} %tokens.1, s32[16,8]{1,0:T(8,128)} %copy.7.ids, f32[16,8]{1,0:T(8,128)} %copy.8.scores, bf16[3584,512]{1,0:T(8,128)(2,1)} %bitcast.4, bf16[3584,512]{1,0:T(8,128)(2,1)} %bitcast.5, bf16[512,3584]{1,0:T(8,128)(2,1)} %bitcast.6), custom_call_target="tpu_custom_call" | custom-call | tf_op jit(solution)/shard_map/pallas_call | solution.py:337
  104.3 1.5 %copy.9 = bf16[16,2,896]{2,1,0:T(2,128)(2,1)} copy(bf16[16,2,896]{2,0,1:T(8,128)(2,1)} %bitcast.7) | data formatting | bytes 114688 | tf_op jit(solution)/shard_map/transpose | solution.py:347

commit v2 on v1

--- a/solution.py
+++ b/solution.py
@@ -21,6 +21,11 @@
 GROUPS = ((0,), (1, -1), (2, -2), (3, -3), (4,))
 START = (0, 1, 3, 5, 7)
 NG = len(GROUPS)
+SEQUENCE = (
+    "r0", "p0", "r1", "s0", "p1", "r2", "p2", "s1", "g0", "r3", "p3", "s2",
+    "r4", "p4", "g1", "s3", "s4", "g2", "g3", "g4", "d4", "d3", "a4", "d2",
+    "a3", "d1", "c4", "a2", "d0", "c3", "a1", "c2", "a0", "c1", "c0",
+)
 N_REMOTE = 128
 N_LOCAL = 32
 
@@ -31,7 +36,7 @@
 
 def kernel(
     tokens, ids, scores, wg_hbm, wu_hbm, wd_hbm, out,
-    w_gu, w_d, tok, slots, relay, x, own_gu, send_gu, recv_gu, hid, y, xr, zsum, yr, relay2,
+    w_gu, w_d, tok, slots, x, own_gu, send_gu, recv_gu, hid, y, xr, zsum, yr,
     mix, zs, zr, f_own, f_send, f_recv,
     send_sem, recv_sem, local_sem,
 ):
@@ -77,8 +82,8 @@
         return pl.ds(pl.multiple_of(b * BLOCK, BLOCK), BLOCK)
 
     barrier = pltpu.get_barrier_semaphore()
-    peers = [at_z(o) for o in range(1, NZ)] + [at_y(1), at_y(-1), at_x(1, d), at_x(-1, d)]
-    peers += [at_x(2, d), at_x(2, 1 - d), at_x(0, 1 - d)]
+    peers = [at_z(o) for o in range(1, NZ)] + [at_y(1), at_y(2), at_y(-1)]
+    peers += [at_x(1, d), at_x(-1, d), at_x(2, d), at_x(2, 1 - d), at_x(0, 1 - d)]
     for peer in peers:
         pl.semaphore_signal(barrier, inc=1, device_id=peer, device_id_type=MESH)
 
@@ -89,20 +94,26 @@
     move("t0", tokens.at[:, half_quarter(d, par)], tok.at[mine, pl.ds(0, Q)])
     move("t1", tokens.at[:, half_quarter(d, par + 2)], tok.at[mine, pl.ds(Q, Q)])
 
-    lane = lax.broadcasted_iota(jnp.int32, (BLOCK, 128), 1)
+    row = lax.broadcasted_iota(jnp.int32, (128, BLOCK), 0)
     chosen, rs = ids[...], scores[...]
-    w = (2.5 * rs / jnp.sum(rs, axis=1, keepdims=True)).astype(BF16).astype(F32)
-    hot = jnp.zeros((BLOCK, 128), F32)
-    weight = jnp.zeros((BLOCK, 128), F32)
+    w = (2.5 * rs / jnp.sum(rs, axis=0, keepdims=True)).astype(BF16).astype(F32)
+    hot = jnp.zeros((128, BLOCK), F32)
+    weight = jnp.zeros((128, BLOCK), F32)
     for k in range(TOP):
-        ek = chosen[:, k:k + 1]
-        hot += jnp.where(ek == lane, 1.0, 0.0)
-        weight += jnp.where(ek + 32 == lane, w[:, k:k + 1], 0.0)
-    lower = jnp.where(
+        ek = chosen[k:k + 1, :]
+        hot += jnp.where(ek == row, 1.0, 0.0)
+        weight += jnp.where(ek + 32 == row, w[k:k + 1, :], 0.0)
+    before = jnp.where(
         lax.broadcasted_iota(jnp.int32, (BLOCK, BLOCK), 0)
-        > lax.broadcasted_iota(jnp.int32, (BLOCK, BLOCK), 1), 1.0, 0.0)
-    earlier = jnp.dot(lower.astype(BF16), hot.astype(BF16), preferred_element_type=F32)
-    table = jnp.where(hot > 0.0, earlier + 1.0, 0.0) + weight
+        < lax.broadcasted_iota(jnp.int32, (BLOCK, BLOCK), 1), 1.0, 0.0)
+    earlier = jnp.dot(hot.astype(BF16), before.astype(BF16), preferred_element_type=F32)
+    turned = jnp.where(hot > 0.0, earlier + 1.0, 0.0) + weight
+    eye = jnp.where(
+        lax.broadcasted_iota(jnp.int32, (128, 128), 0)
+        == lax.broadcasted_iota(jnp.int32, (128, 128), 1), 1.0, 0.0)
+    table = lax.dot_general(
+        turned.astype(BF16), eye.astype(BF16), (((0,), (0,)), ((), ())),
+        preferred_element_type=F32)
     tok[mine, pl.ds(W2, 128)] = table.astype(BF16)
 
     pl.semaphore_wait(barrier, len(peers))
@@ -123,8 +134,7 @@
         n = len(GROUPS[g])
         return n, 64 * START[g], 16 * n
 
-    def gather_and_place(g):
-        n, base, m = span(g)
+    def ring(g):
         if g == 0:
             send(("z", -1), chunk(0), chunk(-1), at_z(1))
             send(("z", 1), chunk(0), chunk(1), at_z(-1))
@@ -140,6 +150,9 @@
         else:
             arrived(("z", "a"))
             arrived(("z", "b"))
+
+    def place_rows(g):
+        n, base, m = span(g)
         first = 32 * START[g]
         tab = tok[first:first + 32 * n, W2:]
         col = lax.broadcasted_iota(jnp.int32, (128, 4 * m), 1)
@@ -168,21 +181,11 @@
         def place(c, k):
             return x.at[pl.ds(base + c * m, m), qs[k]]
 
-        rl = pl.ds(16 * START[g], m)
-        send(("r", g, 0), part(2, lo), relay.at[0, rl], at_y(1))
-        send(("r", g, 1), part(2, hi), relay.at[1, rl], at_y(-1))
         for k, half in enumerate((lo, hi)):
+            send(("y2", g, k), part(2, half), place(2, k), at_y(2))
             send(("y1", g, k), part(1, half), place(3, k), at_y(1))
             send(("y3", g, k), part(3, half), place(1, k), at_y(-1))
             move(("y0", g, k), part(0, half), place(0, k))
-
-    def relay_rows(g):
-        n, base, m = span(g)
-        rl = pl.ds(16 * START[g], m)
-        qs = (quarter(par), quarter(par + 2))
-        for k, step in ((0, 1), (1, -1)):
-            arrived(("r", g, k))
-            send(("y2", g, k), relay.at[k, rl], x.at[pl.ds(base + 2 * m, m), qs[k]], at_y(step))
 
     def swap_halves(g):
         n, base, m = span(g)
@@ -200,13 +203,14 @@
         if g == 0:
             local["wg"].wait()
             local["wu"].wait()
+            local["wd"].wait()
         for k in range(2):
             arrived(("x", g, k))
 
         def tile(i, carry):
             cols = pl.ds(pl.multiple_of(i * 256, 256), 256)
             part = jnp.dot(x[base:base + 4 * m, :], w_gu[:, cols], preferred_element_type=F32)
-            own_gu[g % 2, 0:4 * m, cols] = part
+            own_gu[g, 0:4 * m, cols] = part
             send_gu[base:base + 4 * m, cols] = part.astype(BF16)
             return carry
 
@@ -216,10 +220,8 @@
 
     def down(g):
         n, base, m = span(g)
-        if g == 0:
-            local["wd"].wait()
         arrived(("gu", g))
-        total = own_gu[g % 2, 0:4 * m, :] + recv_gu[base:base + 4 * m, :].astype(F32)
+        total = own_gu[g, 0:4 * m, :] + recv_gu[base:base + 4 * m, :].astype(F32)
         gate, up = total[:, :FFQ], total[:, FFQ:]
         hid[0:4 * m, :] = (gate / (1.0 + jnp.exp(-gate)) * up).astype(BF16)
 
@@ -241,30 +243,19 @@
             mine_y = y[base:base + 4 * m, quarter(par + 2 * k)].astype(F32)
             zsum[base:base + 4 * m, k * Q:(k + 1) * Q] = (
                 mine_y + xr[k, base:base + 4 * m, :].astype(F32)).astype(BF16)
-        lo, hi = pl.ds(0, Q), pl.ds(Q, Q)
-        rl = pl.ds(16 * START[g], m)
 
         def rows(c):
             return pl.ds(base + c * m, m)
 
-        send(("s", g, 0), zsum.at[rows(2), lo], relay2.at[0, rl], at_y(1))
-        send(("s", g, 1), zsum.at[rows(2), hi], relay2.at[1, rl], at_y(-1))
+        send(("v2", g), zsum.at[rows(2)], yr.at[rows(2)], at_y(2))
         send(("v1", g), zsum.at[rows(1)], yr.at[rows(3)], at_y(1))
         send(("v3", g), zsum.at[rows(3)], yr.at[rows(1)], at_y(-1))
         move(("v0", g), zsum.at[rows(0)], yr.at[rows(0)])
 
-    def relay_results(g):
-        n, base, m = span(g)
-        rl = pl.ds(16 * START[g], m)
-        rows = pl.ds(base + 2 * m, m)
-        for k, step in ((0, 1), (1, -1)):
-            arrived(("s", g, k))
-            send(("v2", g, k), relay2.at[k, rl], yr.at[rows, pl.ds(k * Q, Q)], at_y(step))
-
     def combine(g):
         n, base, m = span(g)
         local[("v0", g)].wait()
-        for key in (("v1", g), ("v3", g), ("v2", g, 0), ("v2", g, 1)):
+        for key in (("v1", g), ("v3", g), ("v2", g)):
             arrived(key)
         first = 32 * START[g]
         part = jnp.dot(mix[first:first + 32 * n, 0:4 * m], yr[base:base + 4 * m, :],
@@ -275,14 +266,12 @@
                 send(("w", o), zs.at[pl.ds(32 * place_of(o), 32)],
                      zr.at[pl.ds(32 * place_of(-o), 32)], at_z(o))
 
-    stages = (
-        (gather_and_place, 0), (gate_up, 2), (relay_rows, 0), (down, 2),
-        (add_and_return, 3), (swap_halves, 0), (relay_results, 3), (combine, 4),
-    )
-    for s in range(NG + 4):
-        for stage, lag in stages:
-            if 0 <= s - lag < NG:
-                stage(s - lag)
+    stages = {
+        "r": ring, "p": place_rows, "s": swap_halves, "g": gate_up,
+        "d": down, "a": add_and_return, "c": combine,
+    }
+    for step in SEQUENCE:
+        stages[step[0]](int(step[1]))
 
     total = zs[0:32, :].astype(F32)
     for o in ORDER[1:]:
@@ -313,9 +302,8 @@
         pltpu.VMEM((FFQ, HALF), BF16),
         pltpu.VMEM((32 * NZ, W2 + 128), BF16),
         pltpu.VMEM((ROWS, W2), BF16),
-        pltpu.VMEM((2, 16 * NZ, Q), BF16),
         pltpu.VMEM((ROWS, HALF), BF16),
-        pltpu.VMEM((2, 128, 2 * FFQ), F32),
+        pltpu.VMEM((NG, 128, 2 * FFQ), F32),
         pltpu.VMEM((ROWS, 2 * FFQ), BF16),
         pltpu.VMEM((ROWS, 2 * FFQ), BF16),
         pltpu.VMEM((128, FFQ), BF16),
@@ -323,7 +311,6 @@
         pltpu.VMEM((2, ROWS, Q), BF16),
         pltpu.VMEM((ROWS, W2), BF16),
         pltpu.VMEM((ROWS, W2), BF16),
-        pltpu.VMEM((2, 16 * NZ, Q), BF16),
         pltpu.VMEM((32 * NZ, 128), BF16),
         pltpu.VMEM((32 * NZ, W2), BF16),
         pltpu.VMEM((32 * NZ, W2), BF16),
@@ -343,7 +330,7 @@
         compiler_params=pltpu.CompilerParams(
             collective_id=0, has_side_effects=True, vmem_limit_bytes=60 * 1024 * 1024
         ),
-    )(tokens, expert_ids, route_scores, gate_weight[0], up_weight[0], down_weight[0])
+    )(tokens, expert_ids.T, route_scores.T, gate_weight[0], up_weight[0], down_weight[0])
     return out.transpose(1, 0, 2)
 
 

time: 106 us -> 92.5 us (0.87)
  Pallas kernels: 102 us -> 90.9 us
  local copies, waits for them, and re-layouts: 4.19 us -> 1.49 us
    pallas_call x1, Pallas kernels: 102 us -> 90.9 us  [on_device(): pl.pallas_call(kernel, out_shape=jax.ShapeDtypeStruct((2, BLOCK, Q), BF16...]
    unnamed x2 -> x0, local copies, waits for them, and re-layouts: 2.7 us -> none
where the time goes in v2:
time: 92.5 us; the launch traced here: 92.4 us
  Pallas kernels  90.9 us (98%)
  local copies, waits for them, and re-layouts  1.49 us (2%)
    pallas_call x1, Pallas kernels, on_device(): pl.pallas_call(kernel, out_shape=jax.ShapeDtypeStruct((2, BLOCK, Q), BF16...  90.9 us

profile of v2, /device:TPU:1, one launch (start us, length us, event | category | flops | bytes accessed | tf_op | source)
XLA Modules:
  0.0 92.4 jit_solution(14302971948159216572)
XLA Ops:
  0.0 90.9 %shard_map.64 = bf16[2,16,896]{2,1,0:T(8,128)(2,1)} custom-call(bf16[16,7168]{1,0:T(8,128)(2,1)} %tokens.1, s32[8,16]{1,0:T(8,128)} %bitcast.10, f32[8,16]{1,0:T(8,128)} %bitcast.11, bf16[3584,512]{1,0:T(8,128)(2,1)} %bitcast.6, bf16[3584,512]{1,0:T(8,128)(2,1)} %bitcast.7, bf16[512,3584]{1,0:T(8,128)(2,1)} %bitcast.8), custom_call_target="tpu_custom_call" | custom-call | tf_op jit(solution)/shard_map/pallas_call | solution.py:324
  90.9 1.5 %copy.7 = bf16[16,2,896]{2,1,0:T(2,128)(2,1)} copy(bf16[16,2,896]{2,0,1:T(8,128)(2,1)} %bitcast.9) | data formatting | bytes 114688 | tf_op jit(solution)/shard_map/transpose | solution.py:334

commit v3 on v2

--- a/solution.py
+++ b/solution.py
@@ -23,8 +23,8 @@
 NG = len(GROUPS)
 SEQUENCE = (
     "r0", "p0", "r1", "s0", "p1", "r2", "p2", "s1", "g0", "r3", "p3", "s2",
-    "r4", "p4", "g1", "s3", "s4", "g2", "g3", "g4", "d4", "d3", "a4", "d2",
-    "a3", "d1", "c4", "a2", "d0", "c3", "a1", "c2", "a0", "c1", "c0",
+    "r4", "p4", "g1", "s3", "g2", "s4", "d2", "g3", "g4", "a2", "d3", "d4",
+    "a3", "c2", "a4", "d1", "c3", "d0", "c4", "a1", "a0", "c1", "c0",
 )
 N_REMOTE = 128
 N_LOCAL = 32

time: 92.5 us -> 91.9 us (level)
  no operation moved by 1% of the time
where the time goes in v3:
time: 91.9 us; the launch traced here: 91.7 us
  Pallas kernels  90.2 us (98%)
  local copies, waits for them, and re-layouts  1.49 us (2%)
    pallas_call x1, Pallas kernels, on_device(): pl.pallas_call(kernel, out_shape=jax.ShapeDtypeStruct((2, BLOCK, Q), BF16...  90.2 us

profile of v3, /device:TPU:1, one launch (start us, length us, event | category | flops | bytes accessed | tf_op | source)
XLA Modules:
  0.0 91.7 jit_solution(7104244964072302726)
XLA Ops:
  0.0 90.2 %shard_map.64 = bf16[2,16,896]{2,1,0:T(8,128)(2,1)} custom-call(bf16[16,7168]{1,0:T(8,128)(2,1)} %tokens.1, s32[8,16]{1,0:T(8,128)} %bitcast.10, f32[8,16]{1,0:T(8,128)} %bitcast.11, bf16[3584,512]{1,0:T(8,128)(2,1)} %bitcast.6, bf16[3584,512]{1,0:T(8,128)(2,1)} %bitcast.7, bf16[512,3584]{1,0:T(8,128)(2,1)} %bitcast.8), custom_call_target="tpu_custom_call" | custom-call | tf_op jit(solution)/shard_map/pallas_call | solution.py:324
  90.2 1.5 %copy.7 = bf16[16,2,896]{2,1,0:T(2,128)(2,1)} copy(bf16[16,2,896]{2,0,1:T(8,128)(2,1)} %bitcast.9) | data formatting | bytes 114688 | tf_op jit(solution)/shard_map/transpose | solution.py:334
